TPU v7x, 512 devices: a whole 4x8x8 slice. The times are simulated.
512 devices in a mesh: aux: 32 (over x_lo, y, core), occ: 16 (over z, x_hi).
Axes of the slice: x: 4 (x_hi: 2, x_lo: 2; x = x_hi * 2 + x_lo), y: 8, z: 8, core: 2. Of those that a mesh axis runs over, the one named last changes fastest.
Arguments:
- half_ints: bfloat16 [2048, 32, 576], P(('aux', 'occ')), may hold values from -6 to 6
- vir_coef: bfloat16 [576, 512], replicated, may hold values from -0.03125 to 0.03125
- occ_energy: float32 [32], replicated, may hold values from -2 to -0.5
- vir_energy: float32 [512], replicated, may hold values from 0.2 to 3
Outputs:
- density: float32 [2048, 32, 512], P('occ', 'aux')
All inputs are finite; a program needn't handle non-finite values.
Results may differ from a plain program's by a relative error of at most 0.0032.
Values may be sent and summed in bfloat16 or wider, within the bound.
No kernel may reach another device: no remote copies, remote signals or barrier semaphores. Data moves between devices by JAX's collectives and lax.ppermute only.
A program may use at most 64 MiB of HBM per device.

v0:
```python
import jax
import jax.numpy as jnp
from jax import lax
from jax.experimental import pallas as pl
from jax.experimental.pallas import tpu as pltpu
from jax.sharding import Mesh
from jax.sharding import PartitionSpec as P


AXES = ("xl", "y4", "yb", "c", "z4", "zb", "xh")
SIZES = (2, 4, 2, 2, 4, 2, 2)
COMPACT = ("xl", "yb", "xh", "zb")
MIB = 1 << 20
VMEM = pl.BlockSpec(memory_space=pltpu.VMEM)
SMEM = pl.BlockSpec(memory_space=pltpu.SMEM)


def exact_rows(source_row, rows):
    wanted = lax.broadcasted_iota(jnp.int32, source_row.shape, 1)
    selection = (wanted == source_row).astype(jnp.bfloat16)
    return jnp.dot(selection, rows, preferred_element_type=jnp.float32).astype(jnp.bfloat16)


def left_orbital(y4, z4, c):
    return ((z4 // 2) * 8 + y4 * 2 + z4 % 2) * 2 + c


def kept_rows(core, half_ref, coef_ref):
    row = lax.broadcasted_iota(jnp.int32, (64, 128), 0)
    half_ints = exact_rows(row % 4 * 32 + row // 4 * 2 + core, half_ref[...])
    return jnp.dot(half_ints, coef_ref[...], preferred_element_type=jnp.float32).astype(jnp.bfloat16)


def own_rows_kernel(where, half_ref, coef_ref, out_ref):
    out_ref[...] = kept_rows(where[3], half_ref, coef_ref)


def three_index_kernel(where, own_ref, got_ref, coef_ref, left_ref, right_ref):
    core = where[3]
    rows = jnp.concatenate([own_ref[...], kept_rows(core, got_ref, coef_ref)])
    row = lax.broadcasted_iota(jnp.int32, (128, 128), 0)
    local, first, second = row % 4 + 64 * ((row // 4 + core) % 2), row // 32, (row // 8) % 4
    y4, z4 = jnp.where(core == 0, first, second), jnp.where(core == 0, second, first)
    left_ref[...] = exact_rows(left_orbital(y4, z4, 0) // 2 * 4 + local, rows)
    right_ref[...] = exact_rows(row // 8 * 4 + local, rows)


def first_stage_kernel(right_ref, left_ref, out_ref):
    for target in range(4):
        out_ref[target, 0:128, :] = right_ref[...]
        out_ref[target, 128:160, :] = left_ref[32 * target : 32 * target + 32, :]


def second_stage_kernel(in_ref, out_ref):
    for target in range(4):
        for source in range(4):
            out_ref[target, 128 * source : 128 * source + 128, :] = in_ref[source, 0:128, :]
            at = 128 + 8 * target
            out_ref[target, 512 + 8 * source : 520 + 8 * source, :] = in_ref[source, at : at + 8, :]


def density_kernel(where, occ_ref, left_ref, own_ref, other_ref, vir_ref, out_ref, coulomb, total):
    core = where[3]
    down = jnp.broadcast_to(vir_ref[...], (512, 512))
    total[...] = down.T + down
    coulomb[...] = jnp.zeros_like(coulomb)

    def own(second):
        return own_ref[second, 0:512, :]

    def other(second):
        at = pl.ds(pl.multiple_of(second * 128, 128), 128)
        return jnp.concatenate([other_ref[first, at, :] for first in range(4)])

    for second in range(4):
        left = jnp.concatenate([left_ref[:, second * 4 + first].reshape(128, 512) for first in range(4)]).T
        coulomb[0] += jnp.dot(left, own(second), preferred_element_type=jnp.float32)
        coulomb[1] += jnp.dot(left, other(second), preferred_element_type=jnp.float32)

    amplitudes = []
    for pick in range(2):
        plain = coulomb[pick]
        flipped = plain.T
        denominator = total[...] - occ_ref[where[0]] - occ_ref[where[1 + pick]]
        amplitudes.append(((2.0 * flipped - plain) / denominator).astype(jnp.bfloat16))

    for second in range(4):
        term = jnp.dot(own(second), amplitudes[0], preferred_element_type=jnp.float32)
        term += jnp.dot(other(second), amplitudes[1], preferred_element_type=jnp.float32)
        term = term.astype(jnp.bfloat16)
        for first in range(4):
            y4, z4 = jnp.where(core == 0, first, second), jnp.where(core == 0, second, first)
            for xl in range(2):
                for yb in range(2):
                    share = xl * 8 + (y4 // 2) * 4 + yb * 2 + y4 % 2
                    at = first * 128 + xl * 64 + yb * 32
                    out_ref[share, pl.ds(pl.multiple_of(z4 * 32, 32), 32), :] = term[at : at + 32]


def sum_kernel(shares, out_ref):
    total = shares[0].astype(jnp.float32)
    for source in range(1, 16):
        total += shares[source].astype(jnp.float32)
    row = lax.broadcasted_iota(jnp.int32, (128, 128), 0)
    local, xh, zb, z4, core = row % 4, (row // 4) % 2, (row // 8) % 2, (row // 16) % 4, row // 64
    source_row = (((z4 * 2 + xh) * 2 + zb) * 2 + core) * 4 + local
    out_ref[...] = exact_rows(source_row, total.astype(jnp.bfloat16))


def call(kernel, shapes, specs, scratch=(), flops=0):
    return pl.pallas_call(
        kernel,
        out_shape=[jax.ShapeDtypeStruct(shape, jnp.bfloat16) for shape in shapes],
        in_specs=specs,
        out_specs=[VMEM] * len(shapes),
        scratch_shapes=list(scratch),
        compiler_params=pltpu.CompilerParams(vmem_limit_bytes=24 * MIB),
        cost_estimate=pl.CostEstimate(flops=flops, bytes_accessed=2 * MIB, transcendentals=0),
    )


def device(**at):
    index = 0
    for name, size in zip(AXES, SIZES):
        index = index * size + at[name]
    return index


def places():
    for index in range(512):
        at, rest = {}, index
        for name, size in zip(AXES[::-1], SIZES[::-1]):
            rest, at[name] = divmod(rest, size)
        yield index, at


def lines(core_along_y):
    groups = []
    for _, at in places():
        axis = "y4" if at["c"] == core_along_y else "z4"
        if at[axis] == 0:
            groups.append([device(**{**at, axis: k}) for k in range(4)])
    return groups


def exchange(rows, axes, groups=None):
    return lax.all_to_all(rows, axes, split_axis=0, concat_axis=0, axis_index_groups=groups, tiled=True)


def to_place():
    return [
        (index, device(**{**at, "xl": at["z4"] // 2, "yb": at["z4"] % 2, "z4": at["xl"] * 2 + at["yb"]}))
        for index, at in places()
    ]


def body(half_ints, vir_coef, occ_energy, vir_energy):
    xl, y4, yb, c, z4, zb, xh = (lax.axis_index(a) for a in AXES)
    pair = (((xl * 2 + yb) * 2 + xh) * 2 + zb) * 2
    where = jnp.stack([left_orbital(y4, z4, c), pair + c, pair + 1 - c, c])
    flattened = half_ints.reshape(128, 576)
    got = lax.ppermute(flattened, "c", [(0, 1), (1, 0)])
    (rows,) = call(own_rows_kernel, [(64, 512)], [SMEM, VMEM, VMEM])(where, flattened, vir_coef)
    to_left, to_right = call(three_index_kernel, [(128, 512)] * 2, [SMEM, VMEM, VMEM, VMEM])(where, rows, got, vir_coef)
    right = exchange(to_right.reshape(16, 8, 512), COMPACT)
    (pieces,) = call(first_stage_kernel, [(4, 160, 512)], [VMEM, VMEM])(right.reshape(128, 512), to_left)
    pieces = exchange(pieces, AXES, lines(0))
    (pieces,) = call(second_stage_kernel, [(4, 544, 512)], [VMEM])(pieces)
    own = exchange(pieces, AXES, lines(1))
    other = lax.ppermute(own, "c", [(0, 1), (1, 0)])
    left = jnp.broadcast_to(own[None, :, 512:], (16, 4, 32, 512)).reshape(16, 128, 512)
    left = exchange(left, COMPACT)
    (partial,) = call(
        density_kernel,
        [(16, 128, 512)],
        [SMEM, SMEM, VMEM, VMEM, VMEM, VMEM],
        [pltpu.VMEM((2, 512, 512), jnp.float32), pltpu.VMEM((512, 512), jnp.float32)],
        flops=4 * 512 * 1024 * 2048,
    )(where, occ_energy, left.reshape(16, 16, 8, 512), own, other, vir_energy.reshape(1, 512))
    shares = exchange(partial, COMPACT)
    (summed,) = call(sum_kernel, [(128, 512)], [VMEM])(shares)
    placed = lax.ppermute(summed, AXES, to_place())
    return placed.astype(jnp.float32).reshape(128, 1, 512)


def solution(mesh):
    fine = Mesh(mesh.devices.reshape(SIZES), AXES)
    return jax.shard_map(
        body,
        mesh=fine,
        in_specs=(P(AXES, None, None), P(), P(), P()),
        out_specs=P(("z4", "zb", "xh"), ("xl", "y4", "yb", "c"), None),
        check_vma=False,
    )
```

profile of v0, /device:TPU:2, one launch (start us, length us, event | category | flops | bytes accessed | tf_op | source)
XLA Modules:
  0.0 161.4 jit_solution(8602737951917883735)
XLA Ops:
  0.0 1.9 %collective-permute-start = (bf16[128,576]{1,0:T(8,128)(2,1)}, bf16[128,576]{1,0:T(8,128)(2,1)S(1)}, u32[]{:S(2)}, u32[]{:S(2)}) collective-permute-start(bf16[128,576]{1,0:T(8,128)(2,1)} %bitcast.14), channel_id=1, source_target_pairs={{0,16},{16,0},{1,17},{17,1},{2,18},{18,2},{3,19},{19,3},{4,20},{20... | collective-permute-start | bytes 442376 | tf_op jit(solution)/shard_map/ppermute | solution.py:162
  2.0 0.1 pad_add_fusion.where
  2.0 0.0 copy-start
  2.0 1.1 copy-done
  3.1 0.0 copy-start.2
  3.1 0.9 copy-done.2
  4.0 0.9 shard_map.46.own_ref
  4.9 0.0 collective-permute-done.got_ref
  4.9 0.0 copy-start.1
  4.9 1.1 copy-done.1
  6.0 1.1 shard_map.47
  7.1 14.7 %all_to_all.25 = bf16[16,8,512]{2,1,0:T(8,128)(2,1)S(1)} all-to-all(bf16[16,8,512]{2,1,0:T(8,128)(2,1)S(1)} %bitcast.16), channel_id=1, replica_groups=mesh['xl'=2,'y4'=4,'yb'=2,'c'=2,'z4'=4,'zb'=2,'xh'=2] {'xl','yb','xh','zb'}, dimensions={0} | all-to-all | bytes 262144 | tf_op jit(solution)/shard_map/all_to_all | solution.py:147
  21.9 18.8 %all_to_all.26.in_ref = bf16[4,160,512]{2,1,0:T(8,128)(2,1)S(1)} all-to-all(bf16[4,160,512]{2,1,0:T(8,128)(2,1)S(1)} %shard_map.48), channel_id=1, replica_groups={{0,64,128,192},{1,65,129,193},{2,66,130,194},{3,67,131,195},{4,68,132,1..., dimensions={0} | all-to-all | bytes 1310720 | tf_op jit(solution)/shard_map/all_to_all | solution.py:147
  40.7 0.1 shard_map.49
  40.8 40.1 %all_to_all.27.own_ref = bf16[4,544,512]{2,1,0:T(8,128)(2,1)S(1)} all-to-all(bf16[4,544,512]{2,1,0:T(8,128)(2,1)S(1)} %shard_map.49), channel_id=1, replica_groups={{0,4,8,12},{1,5,9,13},{2,6,10,14},{3,7,11,15},{16,80,144,208},{17,81,14..., dimensions={0} | all-to-all | bytes 4456448 | tf_op jit(solution)/shard_map/all_to_all | solution.py:147
  80.9 1.6 broadcast_in_dim.9
  82.5 0.0 copy-start.5
  82.5 0.0 copy-start.6
  82.5 5.8 %all-to-all-start.3 = ((bf16[16,128,512]{2,1,0:T(8,128)(2,1)}), bf16[16,128,512]{2,1,0:T(8,128)(2,1)}, u32[]{:S(2)}, u32[]{:S(2)}) async-start(bf16[16,128,512]{2,1,0:T(8,128)(2,1)} %broadcast_in_dim.9), calls=%async_computation.3 | async-start | bytes 4194304 | tf_op jit(solution)/shard_map/all_to_all | solution.py:147
  88.3 1.9 %collective-permute-start.1 = (bf16[4,544,512]{2,1,0:T(8,128)(2,1)S(1)}, bf16[4,544,512]{2,1,0:T(8,128)(2,1)S(1)}, u32[]{:S(2)}, u32[]{:S(2)}) collective-permute-start(bf16[4,544,512]{2,1,0:T(8,128)(2,1)S(1)} %all_to_all.27.own_ref), channel_id=1, source_target_pairs={{0,16},{16,0},{1,17},{17,1},{2,18},{18,2},{3,19},{19,3},{4,20},{20... | collective-permute-start | bytes 6684680 | tf_op jit(solution)/shard_map/ppermute | solution.py:170
  90.2 4.3 %collective-permute-done.1.other_ref = bf16[4,544,512]{2,1,0:T(8,128)(2,1)S(1)} collective-permute-done((bf16[4,544,512]{2,1,0:T(8,128)(2,1)S(1)}, bf16[4,544,512]{2,1,0:T(8,128)(2,1)S(1)}, u32[]{:S(2)}, u32[]{:S(2)}) %collective-permute-start.1) | collective-permute-done | bytes 2228256 | tf_op jit(solution)/shard_map/ppermute | solution.py:170
  94.5 0.0 copy-start.3
  94.5 1.4 copy-done.3
  95.9 15.7 %all-to-all-done.3 = bf16[16,128,512]{2,1,0:T(8,128)(2,1)} async-done(((bf16[16,128,512]{2,1,0:T(8,128)(2,1)}), bf16[16,128,512]{2,1,0:T(8,128)(2,1)}, u32[]{:S(2)}, u32[]{:S(2)}) %all-to-all-start.3) | async-done | bytes 2097184 | tf_op jit(solution)/shard_map/all_to_all | solution.py:147
  111.6 0.0 copy-done.5
  111.6 0.0 copy-done.6
  111.6 0.0 copy-start.4
  111.6 1.6 %copy-done.4 = bf16[4,544,512]{2,1,0:T(8,128)(2,1)S(1)} copy-done((bf16[4,544,512]{2,1,0:T(8,128)(2,1)S(1)}, bf16[4,544,512]{2,1,0:T(8,128)(2,1)}, u32[]{:S(2)}) %copy-start.4) | copy-done | bytes 2228248
  113.2 6.4 %shard_map.50 = bf16[16,128,512]{2,1,0:T(8,128)(2,1)S(1)} custom-call(s32[4]{0:T(128)S(1)} %pad_add_fusion.where, f32[32]{0:T(128)S(1)} %copy-done.6, bf16[16,16,8,512]{3,2,1,0:T(8,128)(2,1)} %bitcast.8.left_ref, bf16[4,544,512]{2,1,0:T(8,128)(2,1)S(1)} %all_to_all.27.own_ref, bf16[4,544,512]{2,1,0:T(8,128)(2,1)S(1)} %copy-done.4, f32[1,512]{1,0:T(1,128)S(1)} %bitcast.17), custom_call_target="tpu_custom_call" | custom-call | flops 4294967296 | bytes 2097152 | tf_op jit(solution)/shard_map/pallas_call | solution.py:173
  119.7 28.7 %all_to_all.28.shares = bf16[16,128,512]{2,1,0:T(8,128)(2,1)S(1)} all-to-all(bf16[16,128,512]{2,1,0:T(8,128)(2,1)S(1)} %shard_map.50), channel_id=1, replica_groups=mesh['xl'=2,'y4'=4,'yb'=2,'c'=2,'z4'=4,'zb'=2,'xh'=2] {'xl','yb','xh','zb'}, dimensions={0} | all-to-all | bytes 4194304 | tf_op jit(solution)/shard_map/all_to_all | solution.py:147
  148.3 0.4 shard_map.51
  148.8 2.2 %collective-permute-start.2 = (bf16[128,512]{1,0:T(8,128)(2,1)S(1)}, bf16[128,512]{1,0:T(8,128)(2,1)S(1)}, u32[]{:S(2)}, u32[]{:S(2)}) collective-permute-start(bf16[128,512]{1,0:T(8,128)(2,1)S(1)} %shard_map.51), channel_id=1, source_target_pairs={{0,0},{1,1},{2,2},{3,3},{4,32},{5,33},{6,34},{7,35},{8,256},{9,257... | collective-permute-start | bytes 393224 | tf_op jit(solution)/shard_map/ppermute | solution.py:182
  151.0 9.5 %collective-permute-done.2 = bf16[128,512]{1,0:T(8,128)(2,1)S(1)} collective-permute-done((bf16[128,512]{1,0:T(8,128)(2,1)S(1)}, bf16[128,512]{1,0:T(8,128)(2,1)S(1)}, u32[]{:S(2)}, u32[]{:S(2)}) %collective-permute-start.2) | collective-permute-done | bytes 131104 | tf_op jit(solution)/shard_map/ppermute | solution.py:182
  160.5 1.0 copy.5
  (3 shorter events, 0.1 us)
Async XLA Ops:
  0.0 4.9 %collective-permute-start = (bf16[128,576]{1,0:T(8,128)(2,1)}, bf16[128,576]{1,0:T(8,128)(2,1)S(1)}, u32[]{:S(2)}, u32[]{:S(2)}) collective-permute-start(bf16[128,576]{1,0:T(8,128)(2,1)} %bitcast.14), channel_id=1, source_target_pairs={{0,16},{16,0},{1,17},{17,1},{2,18},{18,2},{3,19},{19,3},{4,20},{20... | collective-permute-start | bytes 442376 | tf_op jit(solution)/shard_map/ppermute | solution.py:162
  2.0 1.1 copy-start
  3.1 0.9 copy-start.2
  4.9 1.1 copy-start.1
  82.5 29.1 %copy-start.5 = (f32[512]{0:T(512)S(1)}, f32[512]{0:T(512)}, u32[]{:S(2)}) copy-start(f32[512]{0:T(512)} %param.7) | copy-start | bytes 6148
  82.5 29.1 %copy-start.6 = (f32[32]{0:T(128)S(1)}, f32[32]{0:T(128)}, u32[]{:S(2)}) copy-start(f32[32]{0:T(128)} %occ_ref.1) | copy-start | bytes 388
  82.5 29.1 %all-to-all-start.3 = ((bf16[16,128,512]{2,1,0:T(8,128)(2,1)}), bf16[16,128,512]{2,1,0:T(8,128)(2,1)}, u32[]{:S(2)}, u32[]{:S(2)}) async-start(bf16[16,128,512]{2,1,0:T(8,128)(2,1)} %broadcast_in_dim.9), calls=%async_computation.3 | async-start | bytes 4194304 | tf_op jit(solution)/shard_map/all_to_all | solution.py:147
  88.3 6.2 %collective-permute-start.1 = (bf16[4,544,512]{2,1,0:T(8,128)(2,1)S(1)}, bf16[4,544,512]{2,1,0:T(8,128)(2,1)S(1)}, u32[]{:S(2)}, u32[]{:S(2)}) collective-permute-start(bf16[4,544,512]{2,1,0:T(8,128)(2,1)S(1)} %all_to_all.27.own_ref), channel_id=1, source_target_pairs={{0,16},{16,0},{1,17},{17,1},{2,18},{18,2},{3,19},{19,3},{4,20},{20... | collective-permute-start | bytes 6684680 | tf_op jit(solution)/shard_map/ppermute | solution.py:170
  94.5 1.4 copy-start.3
  111.6 1.6 %copy-start.4 = (bf16[4,544,512]{2,1,0:T(8,128)(2,1)S(1)}, bf16[4,544,512]{2,1,0:T(8,128)(2,1)}, u32[]{:S(2)}) copy-start(bf16[4,544,512]{2,1,0:T(8,128)(2,1)} %copy-done.3) | copy-start | bytes 6684676
  148.8 11.7 %collective-permute-start.2 = (bf16[128,512]{1,0:T(8,128)(2,1)S(1)}, bf16[128,512]{1,0:T(8,128)(2,1)S(1)}, u32[]{:S(2)}, u32[]{:S(2)}) collective-permute-start(bf16[128,512]{1,0:T(8,128)(2,1)S(1)} %shard_map.51), channel_id=1, source_target_pairs={{0,0},{1,1},{2,2},{3,3},{4,32},{5,33},{6,34},{7,35},{8,256},{9,257... | collective-permute-start | bytes 393224 | tf_op jit(solution)/shard_map/ppermute | solution.py:182
where the time goes:
time: 162 us; the launch traced here: 161 us
  blocking collectives  102 us (63%)
  waiting for transfers between devices  29.5 us (18%)
  starting transfers between devices  11.8 us (7%)
  Pallas kernels  9.06 us (6%)
  local copies, waits for them, and re-layouts  8.59 us (5%)
    all_to_all x4, blocking collectives, exchange(): lax.all_to_all(rows, axes, split_axis=0, concat_axis=0, axis_index_groups...  102 us
    all_to_all x1, waiting for transfers between devices, exchange(): lax.all_to_all(rows, axes, split_axis=0, concat_axis=0, axis_index_groups...  15.7 us
    ppermute x1, waiting for transfers between devices, body(): placed = lax.ppermute(summed, AXES, to_place())  9.47 us
    pallas_call x1, Pallas kernels, body(): call(density_kernel, [(16, 128, 512)], [SMEM, SMEM, VMEM, VMEM, VMEM, VME...  6.45 us
    unnamed x14, local copies, waits for them, and re-layouts  6.05 us
    all_to_all x1, starting transfers between devices, exchange(): lax.all_to_all(rows, axes, split_axis=0, concat_axis=0, axis_index_groups...  5.8 us
    ppermute x1, waiting for transfers between devices, body(): other = lax.ppermute(own, 'c', [(0, 1), (1, 0)])  4.31 us
  transfers between devices with their start and end apart: 4, of which 3 were waited for; matrix products, arithmetic and copies ran while one was open for 0% of the time, Pallas kernels for 1%

commit v1 on v0

--- a/solution.py
+++ b/solution.py
@@ -1,3 +1,5 @@
+import itertools
+
 import jax
 import jax.numpy as jnp
 from jax import lax
@@ -92,7 +94,7 @@
             y4, z4 = jnp.where(core == 0, first, second), jnp.where(core == 0, second, first)
             for xl in range(2):
                 for yb in range(2):
-                    share = xl * 8 + (y4 // 2) * 4 + yb * 2 + y4 % 2
+                    share = xl * 8 + (y4 // 2) * 4 + (yb ^ (y4 // 2)) * 2 + y4 % 2
                     at = first * 128 + xl * 64 + yb * 32
                     out_ref[share, pl.ds(pl.multiple_of(z4 * 32, 32), 32), :] = term[at : at + 32]
 
@@ -103,7 +105,7 @@
         total += shares[source].astype(jnp.float32)
     row = lax.broadcasted_iota(jnp.int32, (128, 128), 0)
     local, xh, zb, z4, core = row % 4, (row // 4) % 2, (row // 8) % 2, (row // 16) % 4, row // 64
-    source_row = (((z4 * 2 + xh) * 2 + zb) * 2 + core) * 4 + local
+    source_row = (((z4 * 2 + xh) * 2 + (zb ^ (z4 // 2))) * 2 + core) * 4 + local
     out_ref[...] = exact_rows(source_row, total.astype(jnp.bfloat16))
 
 
@@ -134,12 +136,29 @@
         yield index, at
 
 
+def on_line(at, axis, k):
+    bit = {"y4": "yb", "z4": "zb"}[axis]
+    return device(**{**at, axis: k, bit: at[bit] ^ k // 2})
+
+
 def lines(core_along_y):
     groups = []
     for _, at in places():
         axis = "y4" if at["c"] == core_along_y else "z4"
         if at[axis] == 0:
-            groups.append([device(**{**at, axis: k}) for k in range(4)])
+            groups.append([on_line(at, axis, k) for k in range(4)])
+    return groups
+
+
+def compact():
+    groups = []
+    for y4, c, z4 in itertools.product(range(4), range(2), range(4)):
+        groups.append(
+            [
+                device(xl=xl, y4=y4, yb=y ^ y4 // 2, c=c, z4=z4, zb=z ^ z4 // 2, xh=xh)
+                for xl, y, xh, z in itertools.product(range(2), repeat=4)
+            ]
+        )
     return groups
 
 
@@ -156,20 +175,20 @@
 
 def body(half_ints, vir_coef, occ_energy, vir_energy):
     xl, y4, yb, c, z4, zb, xh = (lax.axis_index(a) for a in AXES)
-    pair = (((xl * 2 + yb) * 2 + xh) * 2 + zb) * 2
+    pair = (((xl * 2 + (yb ^ y4 // 2)) * 2 + xh) * 2 + (zb ^ z4 // 2)) * 2
     where = jnp.stack([left_orbital(y4, z4, c), pair + c, pair + 1 - c, c])
     flattened = half_ints.reshape(128, 576)
     got = lax.ppermute(flattened, "c", [(0, 1), (1, 0)])
     (rows,) = call(own_rows_kernel, [(64, 512)], [SMEM, VMEM, VMEM])(where, flattened, vir_coef)
     to_left, to_right = call(three_index_kernel, [(128, 512)] * 2, [SMEM, VMEM, VMEM, VMEM])(where, rows, got, vir_coef)
-    right = exchange(to_right.reshape(16, 8, 512), COMPACT)
+    right = exchange(to_right.reshape(16, 8, 512), AXES, compact())
     (pieces,) = call(first_stage_kernel, [(4, 160, 512)], [VMEM, VMEM])(right.reshape(128, 512), to_left)
     pieces = exchange(pieces, AXES, lines(0))
     (pieces,) = call(second_stage_kernel, [(4, 544, 512)], [VMEM])(pieces)
     own = exchange(pieces, AXES, lines(1))
     other = lax.ppermute(own, "c", [(0, 1), (1, 0)])
     left = jnp.broadcast_to(own[None, :, 512:], (16, 4, 32, 512)).reshape(16, 128, 512)
-    left = exchange(left, COMPACT)
+    left = exchange(left, AXES, compact())
     (partial,) = call(
         density_kernel,
         [(16, 128, 512)],

time: 162 us -> 161 us (level)
  the two profiles are of different devices: /device:TPU:2 before, /device:TPU:70 now
where the time goes in v1:
time: 161 us; the launch traced here: 160 us
  blocking collectives  97.7 us (61%)
  waiting for transfers between devices  32 us (20%)
  starting transfers between devices  12.6 us (8%)
  Pallas kernels  9.07 us (6%)
  local copies, waits for them, and re-layouts  8.59 us (5%)
    all_to_all x4, blocking collectives, exchange(): lax.all_to_all(rows, axes, split_axis=0, concat_axis=0, axis_index_groups...  97.7 us
    all_to_all x1, waiting for transfers between devices, exchange(): lax.all_to_all(rows, axes, split_axis=0, concat_axis=0, axis_index_groups...  15.9 us
    ppermute x1, waiting for transfers between devices, body(): placed = lax.ppermute(summed, AXES, to_place())  11.8 us
    pallas_call x1, Pallas kernels, body(): call(density_kernel, [(16, 128, 512)], [SMEM, SMEM, VMEM, VMEM, VMEM, VME...  6.45 us
    all_to_all x1, starting transfers between devices, exchange(): lax.all_to_all(rows, axes, split_axis=0, concat_axis=0, axis_index_groups...  6.42 us
    unnamed x14, local copies, waits for them, and re-layouts  6.05 us
    ppermute x1, waiting for transfers between devices, body(): other = lax.ppermute(own, 'c', [(0, 1), (1, 0)])  4.31 us
  transfers between devices with their start and end apart: 4, of which 3 were waited for; matrix products, arithmetic and copies ran while one was open for 0% of the time, Pallas kernels for 1%

profile of v1, /device:TPU:70, one launch (start us, length us, event | category | flops | bytes accessed | tf_op | source)
XLA Modules:
  0.0 160.3 jit_solution(13590657575932146173)
XLA Ops:
  0.0 1.9 %collective-permute-start = (bf16[128,576]{1,0:T(8,128)(2,1)}, bf16[128,576]{1,0:T(8,128)(2,1)S(1)}, u32[]{:S(2)}, u32[]{:S(2)}) collective-permute-start(bf16[128,576]{1,0:T(8,128)(2,1)} %bitcast.14), channel_id=1, source_target_pairs={{0,16},{16,0},{1,17},{17,1},{2,18},{18,2},{3,19},{19,3},{4,20},{20... | collective-permute-start | bytes 442376 | tf_op jit(solution)/shard_map/ppermute | solution.py:181
  2.0 0.1 pad_add_fusion.where
  2.0 0.0 copy-start
  2.0 1.1 copy-done
  3.1 0.0 copy-start.2
  3.1 0.9 copy-done.2
  4.0 0.9 shard_map.46.own_ref
  4.9 0.0 collective-permute-done.got_ref
  4.9 0.0 copy-start.1
  4.9 1.1 copy-done.1
  6.0 1.1 shard_map.47
  7.1 12.4 %all_to_all.25 = bf16[16,8,512]{2,1,0:T(8,128)(2,1)S(1)} all-to-all(bf16[16,8,512]{2,1,0:T(8,128)(2,1)S(1)} %bitcast.16), channel_id=1, replica_groups={{0,2,1,3,32,34,33,35,256,258,257,259,288,290,289,291},{4,6,5,7,36,38,37..., dimensions={0} | all-to-all | bytes 262144 | tf_op jit(solution)/shard_map/all_to_all | solution.py:166
  19.6 18.6 %all_to_all.26.in_ref = bf16[4,160,512]{2,1,0:T(8,128)(2,1)S(1)} all-to-all(bf16[4,160,512]{2,1,0:T(8,128)(2,1)S(1)} %shard_map.48), channel_id=1, replica_groups={{0,64,160,224},{1,65,161,225},{2,66,162,226},{3,67,163,227},{4,68,164,2..., dimensions={0} | all-to-all | bytes 1310720 | tf_op jit(solution)/shard_map/all_to_all | solution.py:166
  38.1 0.1 shard_map.49
  38.3 39.0 %all_to_all.27.own_ref = bf16[4,544,512]{2,1,0:T(8,128)(2,1)S(1)} all-to-all(bf16[4,544,512]{2,1,0:T(8,128)(2,1)S(1)} %shard_map.49), channel_id=1, replica_groups={{0,4,10,14},{1,5,11,15},{2,6,8,12},{3,7,9,13},{16,80,176,240},{17,81,17..., dimensions={0} | all-to-all | bytes 4456448 | tf_op jit(solution)/shard_map/all_to_all | solution.py:166
  77.3 1.6 broadcast_in_dim.9
  78.8 0.0 copy-start.5
  78.8 0.0 copy-start.6
  78.8 6.4 %all-to-all-start.3 = ((bf16[16,128,512]{2,1,0:T(8,128)(2,1)}), bf16[16,128,512]{2,1,0:T(8,128)(2,1)}, u32[]{:S(2)}, u32[]{:S(2)}) async-start(bf16[16,128,512]{2,1,0:T(8,128)(2,1)} %broadcast_in_dim.9), calls=%async_computation.3 | async-start | bytes 4194304 | tf_op jit(solution)/shard_map/all_to_all | solution.py:166
  85.3 1.9 %collective-permute-start.1 = (bf16[4,544,512]{2,1,0:T(8,128)(2,1)S(1)}, bf16[4,544,512]{2,1,0:T(8,128)(2,1)S(1)}, u32[]{:S(2)}, u32[]{:S(2)}) collective-permute-start(bf16[4,544,512]{2,1,0:T(8,128)(2,1)S(1)} %all_to_all.27.own_ref), channel_id=1, source_target_pairs={{0,16},{16,0},{1,17},{17,1},{2,18},{18,2},{3,19},{19,3},{4,20},{20... | collective-permute-start | bytes 6684680 | tf_op jit(solution)/shard_map/ppermute | solution.py:189
  87.2 4.3 %collective-permute-done.1.other_ref = bf16[4,544,512]{2,1,0:T(8,128)(2,1)S(1)} collective-permute-done((bf16[4,544,512]{2,1,0:T(8,128)(2,1)S(1)}, bf16[4,544,512]{2,1,0:T(8,128)(2,1)S(1)}, u32[]{:S(2)}, u32[]{:S(2)}) %collective-permute-start.1) | collective-permute-done | bytes 2228256 | tf_op jit(solution)/shard_map/ppermute | solution.py:189
  91.5 0.0 copy-start.3
  91.5 1.4 copy-done.3
  92.9 15.9 %all-to-all-done.3 = bf16[16,128,512]{2,1,0:T(8,128)(2,1)} async-done(((bf16[16,128,512]{2,1,0:T(8,128)(2,1)}), bf16[16,128,512]{2,1,0:T(8,128)(2,1)}, u32[]{:S(2)}, u32[]{:S(2)}) %all-to-all-start.3) | async-done | bytes 2097184 | tf_op jit(solution)/shard_map/all_to_all | solution.py:166
  108.8 0.0 copy-done.5
  108.8 0.0 copy-done.6
  108.8 0.0 copy-start.4
  108.8 1.6 %copy-done.4 = bf16[4,544,512]{2,1,0:T(8,128)(2,1)S(1)} copy-done((bf16[4,544,512]{2,1,0:T(8,128)(2,1)S(1)}, bf16[4,544,512]{2,1,0:T(8,128)(2,1)}, u32[]{:S(2)}) %copy-start.4) | copy-done | bytes 2228248
  110.4 6.4 %shard_map.50 = bf16[16,128,512]{2,1,0:T(8,128)(2,1)S(1)} custom-call(s32[4]{0:T(128)S(1)} %pad_add_fusion.where, f32[32]{0:T(128)S(1)} %copy-done.6, bf16[16,16,8,512]{3,2,1,0:T(8,128)(2,1)} %bitcast.8.left_ref, bf16[4,544,512]{2,1,0:T(8,128)(2,1)S(1)} %all_to_all.27.own_ref, bf16[4,544,512]{2,1,0:T(8,128)(2,1)S(1)} %copy-done.4, f32[1,512]{1,0:T(1,128)S(1)} %bitcast.17), custom_call_target="tpu_custom_call" | custom-call | flops 4294967296 | bytes 2097152 | tf_op jit(solution)/shard_map/pallas_call | solution.py:192
  116.9 27.8 %all_to_all.28.shares = bf16[16,128,512]{2,1,0:T(8,128)(2,1)S(1)} all-to-all(bf16[16,128,512]{2,1,0:T(8,128)(2,1)S(1)} %shard_map.50), channel_id=1, replica_groups=mesh['xl'=2,'y4'=4,'yb'=2,'c'=2,'z4'=4,'zb'=2,'xh'=2] {'xl','yb','xh','zb'}, dimensions={0} | all-to-all | bytes 4194304 | tf_op jit(solution)/shard_map/all_to_all | solution.py:166
  144.6 0.4 shard_map.51
  145.1 2.4 %collective-permute-start.2 = (bf16[128,512]{1,0:T(8,128)(2,1)S(1)}, bf16[128,512]{1,0:T(8,128)(2,1)S(1)}, u32[]{:S(2)}, u32[]{:S(2)}) collective-permute-start(bf16[128,512]{1,0:T(8,128)(2,1)S(1)} %shard_map.51), channel_id=1, source_target_pairs={{0,0},{1,1},{2,2},{3,3},{4,32},{5,33},{6,34},{7,35},{8,256},{9,257... | collective-permute-start | bytes 393224 | tf_op jit(solution)/shard_map/ppermute | solution.py:201
  147.5 11.8 %collective-permute-done.2 = bf16[128,512]{1,0:T(8,128)(2,1)S(1)} collective-permute-done((bf16[128,512]{1,0:T(8,128)(2,1)S(1)}, bf16[128,512]{1,0:T(8,128)(2,1)S(1)}, u32[]{:S(2)}, u32[]{:S(2)}) %collective-permute-start.2) | collective-permute-done | bytes 131104 | tf_op jit(solution)/shard_map/ppermute | solution.py:201
  159.3 1.0 copy.5
  (3 shorter events, 0.1 us)
Async XLA Ops:
  0.0 4.9 %collective-permute-start = (bf16[128,576]{1,0:T(8,128)(2,1)}, bf16[128,576]{1,0:T(8,128)(2,1)S(1)}, u32[]{:S(2)}, u32[]{:S(2)}) collective-permute-start(bf16[128,576]{1,0:T(8,128)(2,1)} %bitcast.14), channel_id=1, source_target_pairs={{0,16},{16,0},{1,17},{17,1},{2,18},{18,2},{3,19},{19,3},{4,20},{20... | collective-permute-start | bytes 442376 | tf_op jit(solution)/shard_map/ppermute | solution.py:181
  2.0 1.1 copy-start
  3.1 0.9 copy-start.2
  4.9 1.1 copy-start.1
  78.8 29.9 %copy-start.5 = (f32[512]{0:T(512)S(1)}, f32[512]{0:T(512)}, u32[]{:S(2)}) copy-start(f32[512]{0:T(512)} %param.7) | copy-start | bytes 6148
  78.8 29.9 %copy-start.6 = (f32[32]{0:T(128)S(1)}, f32[32]{0:T(128)}, u32[]{:S(2)}) copy-start(f32[32]{0:T(128)} %occ_ref.1) | copy-start | bytes 388
  78.8 29.9 %all-to-all-start.3 = ((bf16[16,128,512]{2,1,0:T(8,128)(2,1)}), bf16[16,128,512]{2,1,0:T(8,128)(2,1)}, u32[]{:S(2)}, u32[]{:S(2)}) async-start(bf16[16,128,512]{2,1,0:T(8,128)(2,1)} %broadcast_in_dim.9), calls=%async_computation.3 | async-start | bytes 4194304 | tf_op jit(solution)/shard_map/all_to_all | solution.py:166
  85.3 6.2 %collective-permute-start.1 = (bf16[4,544,512]{2,1,0:T(8,128)(2,1)S(1)}, bf16[4,544,512]{2,1,0:T(8,128)(2,1)S(1)}, u32[]{:S(2)}, u32[]{:S(2)}) collective-permute-start(bf16[4,544,512]{2,1,0:T(8,128)(2,1)S(1)} %all_to_all.27.own_ref), channel_id=1, source_target_pairs={{0,16},{16,0},{1,17},{17,1},{2,18},{18,2},{3,19},{19,3},{4,20},{20... | collective-permute-start | bytes 6684680 | tf_op jit(solution)/shard_map/ppermute | solution.py:189
  91.5 1.4 copy-start.3
  108.8 1.6 %copy-start.4 = (bf16[4,544,512]{2,1,0:T(8,128)(2,1)S(1)}, bf16[4,544,512]{2,1,0:T(8,128)(2,1)}, u32[]{:S(2)}) copy-start(bf16[4,544,512]{2,1,0:T(8,128)(2,1)} %copy-done.3) | copy-start | bytes 6684676
  145.1 14.2 %collective-permute-start.2 = (bf16[128,512]{1,0:T(8,128)(2,1)S(1)}, bf16[128,512]{1,0:T(8,128)(2,1)S(1)}, u32[]{:S(2)}, u32[]{:S(2)}) collective-permute-start(bf16[128,512]{1,0:T(8,128)(2,1)S(1)} %shard_map.51), channel_id=1, source_target_pairs={{0,0},{1,1},{2,2},{3,3},{4,32},{5,33},{6,34},{7,35},{8,256},{9,257... | collective-permute-start | bytes 393224 | tf_op jit(solution)/shard_map/ppermute | solution.py:201

commit v2 on v1

--- a/solution.py
+++ b/solution.py
@@ -94,7 +94,7 @@
             y4, z4 = jnp.where(core == 0, first, second), jnp.where(core == 0, second, first)
             for xl in range(2):
                 for yb in range(2):
-                    share = xl * 8 + (y4 // 2) * 4 + (yb ^ (y4 // 2)) * 2 + y4 % 2
+                    share = xl * 8 + (y4 // 2) * 4 + (yb ^ (y4 // 2)) * 2 + ((y4 % 2) ^ xl ^ where[4])
                     at = first * 128 + xl * 64 + yb * 32
                     out_ref[share, pl.ds(pl.multiple_of(z4 * 32, 32), 32), :] = term[at : at + 32]
 
@@ -168,7 +168,18 @@
 
 def to_place():
     return [
-        (index, device(**{**at, "xl": at["z4"] // 2, "yb": at["z4"] % 2, "z4": at["xl"] * 2 + at["yb"]}))
+        (
+            index,
+            device(
+                **{
+                    **at,
+                    "xl": at["z4"] // 2,
+                    "yb": at["z4"] % 2,
+                    "z4": at["xl"] * 2 + at["yb"],
+                    "zb": at["zb"] ^ at["xl"] ^ at["z4"] // 2,
+                }
+            ),
+        )
         for index, at in places()
     ]
 
@@ -176,7 +187,7 @@
 def body(half_ints, vir_coef, occ_energy, vir_energy):
     xl, y4, yb, c, z4, zb, xh = (lax.axis_index(a) for a in AXES)
     pair = (((xl * 2 + (yb ^ y4 // 2)) * 2 + xh) * 2 + (zb ^ z4 // 2)) * 2
-    where = jnp.stack([left_orbital(y4, z4, c), pair + c, pair + 1 - c, c])
+    where = jnp.stack([left_orbital(y4, z4, c), pair + c, pair + 1 - c, c, z4 // 2])
     flattened = half_ints.reshape(128, 576)
     got = lax.ppermute(flattened, "c", [(0, 1), (1, 0)])
     (rows,) = call(own_rows_kernel, [(64, 512)], [SMEM, VMEM, VMEM])(where, flattened, vir_coef)

time: 161 us -> 160 us (level)
  the two profiles are of different devices: /device:TPU:70 before, /device:TPU:66 now
where the time goes in v2:
time: 160 us
  blocking collectives  98.6 us (62%)
  waiting for transfers between devices  29.9 us (19%)
  starting transfers between devices  13.3 us (8%)
  Pallas kernels  9.07 us (6%)
  local copies, waits for them, and re-layouts  8.68 us (5%)
    all_to_all x4, blocking collectives, exchange(): lax.all_to_all(rows, axes, split_axis=0, concat_axis=0, axis_index_groups...  98.6 us
    all_to_all x1, waiting for transfers between devices, exchange(): lax.all_to_all(rows, axes, split_axis=0, concat_axis=0, axis_index_groups...  15.8 us
    ppermute x1, waiting for transfers between devices, body(): placed = lax.ppermute(summed, AXES, to_place())  9.84 us
    pallas_call x1, Pallas kernels, body(): call(density_kernel, [(16, 128, 512)], [SMEM, SMEM, VMEM, VMEM, VMEM, VME...  6.45 us
    all_to_all x1, starting transfers between devices, exchange(): lax.all_to_all(rows, axes, split_axis=0, concat_axis=0, axis_index_groups...  6.11 us
    unnamed x14, local copies, waits for them, and re-layouts  6.05 us
    ppermute x1, waiting for transfers between devices, body(): other = lax.ppermute(own, 'c', [(0, 1), (1, 0)])  4.31 us
    ppermute x1, starting transfers between devices, body(): placed = lax.ppermute(summed, AXES, to_place())  3.41 us
  transfers between devices with their start and end apart: 4, of which 3 were waited for; matrix products, arithmetic and copies ran while one was open for 0% of the time, Pallas kernels for 1%

profile of v2, /device:TPU:66, one launch (start us, length us, event | category | flops | bytes accessed | tf_op | source)
XLA Modules:
  0.0 159.8 jit_solution(18054210831101759880)
XLA Ops:
  0.0 1.9 %collective-permute-start = (bf16[128,576]{1,0:T(8,128)(2,1)}, bf16[128,576]{1,0:T(8,128)(2,1)S(1)}, u32[]{:S(2)}, u32[]{:S(2)}) collective-permute-start(bf16[128,576]{1,0:T(8,128)(2,1)} %bitcast.15), channel_id=1, source_target_pairs={{0,16},{16,0},{1,17},{17,1},{2,18},{18,2},{3,19},{19,3},{4,20},{20... | collective-permute-start | bytes 442376 | tf_op jit(solution)/shard_map/ppermute | solution.py:192
  2.0 0.1 stack.23.where
  2.0 0.0 copy-start
  2.0 1.1 copy-done
  3.1 0.0 copy-start.2
  3.1 0.9 copy-done.2
  4.0 0.9 shard_map.46.own_ref
  4.9 0.0 collective-permute-done.got_ref
  4.9 0.0 copy-start.1
  4.9 1.1 copy-done.1
  6.0 1.1 shard_map.47
  7.1 12.9 %all_to_all.25 = bf16[16,8,512]{2,1,0:T(8,128)(2,1)S(1)} all-to-all(bf16[16,8,512]{2,1,0:T(8,128)(2,1)S(1)} %bitcast.17), channel_id=1, replica_groups={{0,2,1,3,32,34,33,35,256,258,257,259,288,290,289,291},{4,6,5,7,36,38,37..., dimensions={0} | all-to-all | bytes 262144 | tf_op jit(solution)/shard_map/all_to_all | solution.py:166
  20.1 18.2 %all_to_all.26.in_ref = bf16[4,160,512]{2,1,0:T(8,128)(2,1)S(1)} all-to-all(bf16[4,160,512]{2,1,0:T(8,128)(2,1)S(1)} %shard_map.48), channel_id=1, replica_groups={{0,64,160,224},{1,65,161,225},{2,66,162,226},{3,67,163,227},{4,68,164,2..., dimensions={0} | all-to-all | bytes 1310720 | tf_op jit(solution)/shard_map/all_to_all | solution.py:166
  38.3 0.1 shard_map.49
  38.5 39.2 %all_to_all.27.own_ref = bf16[4,544,512]{2,1,0:T(8,128)(2,1)S(1)} all-to-all(bf16[4,544,512]{2,1,0:T(8,128)(2,1)S(1)} %shard_map.49), channel_id=1, replica_groups={{0,4,10,14},{1,5,11,15},{2,6,8,12},{3,7,9,13},{16,80,176,240},{17,81,17..., dimensions={0} | all-to-all | bytes 4456448 | tf_op jit(solution)/shard_map/all_to_all | solution.py:166
  77.6 1.6 broadcast_in_dim.9
  79.2 0.0 copy-start.5
  79.2 0.0 copy-start.6
  79.2 6.1 %all-to-all-start.3 = ((bf16[16,128,512]{2,1,0:T(8,128)(2,1)}), bf16[16,128,512]{2,1,0:T(8,128)(2,1)}, u32[]{:S(2)}, u32[]{:S(2)}) async-start(bf16[16,128,512]{2,1,0:T(8,128)(2,1)} %broadcast_in_dim.9), calls=%async_computation.3 | async-start | bytes 4194304 | tf_op jit(solution)/shard_map/all_to_all | solution.py:166
  85.3 1.9 %collective-permute-start.1 = (bf16[4,544,512]{2,1,0:T(8,128)(2,1)S(1)}, bf16[4,544,512]{2,1,0:T(8,128)(2,1)S(1)}, u32[]{:S(2)}, u32[]{:S(2)}) collective-permute-start(bf16[4,544,512]{2,1,0:T(8,128)(2,1)S(1)} %all_to_all.27.own_ref), channel_id=1, source_target_pairs={{0,16},{16,0},{1,17},{17,1},{2,18},{18,2},{3,19},{19,3},{4,20},{20... | collective-permute-start | bytes 6684680 | tf_op jit(solution)/shard_map/ppermute | solution.py:200
  87.2 4.3 %collective-permute-done.1.other_ref = bf16[4,544,512]{2,1,0:T(8,128)(2,1)S(1)} collective-permute-done((bf16[4,544,512]{2,1,0:T(8,128)(2,1)S(1)}, bf16[4,544,512]{2,1,0:T(8,128)(2,1)S(1)}, u32[]{:S(2)}, u32[]{:S(2)}) %collective-permute-start.1) | collective-permute-done | bytes 2228256 | tf_op jit(solution)/shard_map/ppermute | solution.py:200
  91.5 0.0 copy-start.3
  91.5 1.4 copy-done.3
  92.9 15.8 %all-to-all-done.3 = bf16[16,128,512]{2,1,0:T(8,128)(2,1)} async-done(((bf16[16,128,512]{2,1,0:T(8,128)(2,1)}), bf16[16,128,512]{2,1,0:T(8,128)(2,1)}, u32[]{:S(2)}, u32[]{:S(2)}) %all-to-all-start.3) | async-done | bytes 2097184 | tf_op jit(solution)/shard_map/all_to_all | solution.py:166
  108.7 0.0 copy-done.5
  108.7 0.0 copy-done.6
  108.7 0.0 copy-start.4
  108.7 1.6 %copy-done.4 = bf16[4,544,512]{2,1,0:T(8,128)(2,1)S(1)} copy-done((bf16[4,544,512]{2,1,0:T(8,128)(2,1)S(1)}, bf16[4,544,512]{2,1,0:T(8,128)(2,1)}, u32[]{:S(2)}) %copy-start.4) | copy-done | bytes 2228248
  110.3 6.4 %shard_map.50 = bf16[16,128,512]{2,1,0:T(8,128)(2,1)S(1)} custom-call(s32[5]{0:T(128)S(1)} %stack.23.where, f32[32]{0:T(128)S(1)} %copy-done.6, bf16[16,16,8,512]{3,2,1,0:T(8,128)(2,1)} %bitcast.9.left_ref, bf16[4,544,512]{2,1,0:T(8,128)(2,1)S(1)} %all_to_all.27.own_ref, bf16[4,544,512]{2,1,0:T(8,128)(2,1)S(1)} %copy-done.4, f32[1,512]{1,0:T(1,128)S(1)} %bitcast.18), custom_call_target="tpu_custom_call" | custom-call | flops 4294967296 | bytes 2097152 | tf_op jit(solution)/shard_map/pallas_call | solution.py:203
  116.8 28.3 %all_to_all.28.shares = bf16[16,128,512]{2,1,0:T(8,128)(2,1)S(1)} all-to-all(bf16[16,128,512]{2,1,0:T(8,128)(2,1)S(1)} %shard_map.50), channel_id=1, replica_groups=mesh['xl'=2,'y4'=4,'yb'=2,'c'=2,'z4'=4,'zb'=2,'xh'=2] {'xl','yb','xh','zb'}, dimensions={0} | all-to-all | bytes 4194304 | tf_op jit(solution)/shard_map/all_to_all | solution.py:166
  145.1 0.4 shard_map.51
  145.5 3.4 %collective-permute-start.2 = (bf16[128,512]{1,0:T(8,128)(2,1)S(1)}, bf16[128,512]{1,0:T(8,128)(2,1)S(1)}, u32[]{:S(2)}, u32[]{:S(2)}) collective-permute-start(bf16[128,512]{1,0:T(8,128)(2,1)S(1)} %shard_map.51), channel_id=1, source_target_pairs={{0,0},{1,1},{2,2},{3,3},{4,32},{5,33},{6,34},{7,35},{8,258},{9,259... | collective-permute-start | bytes 393224 | tf_op jit(solution)/shard_map/ppermute | solution.py:212
  148.9 9.8 %collective-permute-done.2 = bf16[128,512]{1,0:T(8,128)(2,1)S(1)} collective-permute-done((bf16[128,512]{1,0:T(8,128)(2,1)S(1)}, bf16[128,512]{1,0:T(8,128)(2,1)S(1)}, u32[]{:S(2)}, u32[]{:S(2)}) %collective-permute-start.2) | collective-permute-done | bytes 131104 | tf_op jit(solution)/shard_map/ppermute | solution.py:212
  158.8 1.0 copy.5
  (3 shorter events, 0.1 us)
Async XLA Ops:
  0.0 4.9 %collective-permute-start = (bf16[128,576]{1,0:T(8,128)(2,1)}, bf16[128,576]{1,0:T(8,128)(2,1)S(1)}, u32[]{:S(2)}, u32[]{:S(2)}) collective-permute-start(bf16[128,576]{1,0:T(8,128)(2,1)} %bitcast.15), channel_id=1, source_target_pairs={{0,16},{16,0},{1,17},{17,1},{2,18},{18,2},{3,19},{19,3},{4,20},{20... | collective-permute-start | bytes 442376 | tf_op jit(solution)/shard_map/ppermute | solution.py:192
  2.0 1.1 copy-start
  3.1 0.9 copy-start.2
  4.9 1.1 copy-start.1
  79.2 29.5 %copy-start.5 = (f32[512]{0:T(512)S(1)}, f32[512]{0:T(512)}, u32[]{:S(2)}) copy-start(f32[512]{0:T(512)} %param.7) | copy-start | bytes 6148
  79.2 29.5 %copy-start.6 = (f32[32]{0:T(128)S(1)}, f32[32]{0:T(128)}, u32[]{:S(2)}) copy-start(f32[32]{0:T(128)} %occ_ref.1) | copy-start | bytes 388
  79.2 29.5 %all-to-all-start.3 = ((bf16[16,128,512]{2,1,0:T(8,128)(2,1)}), bf16[16,128,512]{2,1,0:T(8,128)(2,1)}, u32[]{:S(2)}, u32[]{:S(2)}) async-start(bf16[16,128,512]{2,1,0:T(8,128)(2,1)} %broadcast_in_dim.9), calls=%async_computation.3 | async-start | bytes 4194304 | tf_op jit(solution)/shard_map/all_to_all | solution.py:166
  85.3 6.2 %collective-permute-start.1 = (bf16[4,544,512]{2,1,0:T(8,128)(2,1)S(1)}, bf16[4,544,512]{2,1,0:T(8,128)(2,1)S(1)}, u32[]{:S(2)}, u32[]{:S(2)}) collective-permute-start(bf16[4,544,512]{2,1,0:T(8,128)(2,1)S(1)} %all_to_all.27.own_ref), channel_id=1, source_target_pairs={{0,16},{16,0},{1,17},{17,1},{2,18},{18,2},{3,19},{19,3},{4,20},{20... | collective-permute-start | bytes 6684680 | tf_op jit(solution)/shard_map/ppermute | solution.py:200
  91.5 1.4 copy-start.3
  108.7 1.6 %copy-start.4 = (bf16[4,544,512]{2,1,0:T(8,128)(2,1)S(1)}, bf16[4,544,512]{2,1,0:T(8,128)(2,1)}, u32[]{:S(2)}) copy-start(bf16[4,544,512]{2,1,0:T(8,128)(2,1)} %copy-done.3) | copy-start | bytes 6684676
  145.5 13.3 %collective-permute-start.2 = (bf16[128,512]{1,0:T(8,128)(2,1)S(1)}, bf16[128,512]{1,0:T(8,128)(2,1)S(1)}, u32[]{:S(2)}, u32[]{:S(2)}) collective-permute-start(bf16[128,512]{1,0:T(8,128)(2,1)S(1)} %shard_map.51), channel_id=1, source_target_pairs={{0,0},{1,1},{2,2},{3,3},{4,32},{5,33},{6,34},{7,35},{8,258},{9,259... | collective-permute-start | bytes 393224 | tf_op jit(solution)/shard_map/ppermute | solution.py:212

commit v3 on v2

--- a/solution.py
+++ b/solution.py
@@ -33,7 +33,8 @@
     return jnp.dot(half_ints, coef_ref[...], preferred_element_type=jnp.float32).astype(jnp.bfloat16)
 
 
-def own_rows_kernel(where, half_ref, coef_ref, out_ref):
+def own_rows_kernel(where, half_ref, coef_ref, out_ref, held_ref):
+    held_ref[...] = coef_ref[...]
     out_ref[...] = kept_rows(where[3], half_ref, coef_ref)
 
 
@@ -190,8 +191,8 @@
     where = jnp.stack([left_orbital(y4, z4, c), pair + c, pair + 1 - c, c, z4 // 2])
     flattened = half_ints.reshape(128, 576)
     got = lax.ppermute(flattened, "c", [(0, 1), (1, 0)])
-    (rows,) = call(own_rows_kernel, [(64, 512)], [SMEM, VMEM, VMEM])(where, flattened, vir_coef)
-    to_left, to_right = call(three_index_kernel, [(128, 512)] * 2, [SMEM, VMEM, VMEM, VMEM])(where, rows, got, vir_coef)
+    rows, held = call(own_rows_kernel, [(64, 512), (576, 512)], [SMEM, VMEM, VMEM])(where, flattened, vir_coef)
+    to_left, to_right = call(three_index_kernel, [(128, 512)] * 2, [SMEM, VMEM, VMEM, VMEM])(where, rows, got, held)
     right = exchange(to_right.reshape(16, 8, 512), AXES, compact())
     (pieces,) = call(first_stage_kernel, [(4, 160, 512)], [VMEM, VMEM])(right.reshape(128, 512), to_left)
     pieces = exchange(pieces, AXES, lines(0))

time: 160 us -> 159 us (level)
    unnamed x14 -> x12, local copies, waits for them, and re-layouts: 6.05 us -> 4.99 us
where the time goes in v3:
time: 159 us
  blocking collectives  98.6 us (62%)
  waiting for transfers between devices  29.9 us (19%)
  starting transfers between devices  13.3 us (8%)
  Pallas kernels  9.11 us (6%)
  local copies, waits for them, and re-layouts  7.62 us (5%)
    all_to_all x4, blocking collectives, exchange(): lax.all_to_all(rows, axes, split_axis=0, concat_axis=0, axis_index_groups...  98.6 us
    all_to_all x1, waiting for transfers between devices, exchange(): lax.all_to_all(rows, axes, split_axis=0, concat_axis=0, axis_index_groups...  15.8 us
    ppermute x1, waiting for transfers between devices, body(): placed = lax.ppermute(summed, AXES, to_place())  9.84 us
    pallas_call x1, Pallas kernels, body(): call(density_kernel, [(16, 128, 512)], [SMEM, SMEM, VMEM, VMEM, VMEM, VME...  6.45 us
    all_to_all x1, starting transfers between devices, exchange(): lax.all_to_all(rows, axes, split_axis=0, concat_axis=0, axis_index_groups...  6.11 us
    unnamed x12, local copies, waits for them, and re-layouts  4.99 us
    ppermute x1, waiting for transfers between devices, body(): other = lax.ppermute(own, 'c', [(0, 1), (1, 0)])  4.31 us
    ppermute x1, starting transfers between devices, body(): placed = lax.ppermute(summed, AXES, to_place())  3.41 us
  transfers between devices with their start and end apart: 4, of which 3 were waited for; matrix products, arithmetic and copies ran while one was open for 0% of the time, Pallas kernels for 1%

profile of v3, /device:TPU:66, one launch (start us, length us, event | category | flops | bytes accessed | tf_op | source)
XLA Modules:
  0.0 158.8 jit_solution(9185369057106356639)
XLA Ops:
  0.0 1.9 %collective-permute-start = (bf16[128,576]{1,0:T(8,128)(2,1)}, bf16[128,576]{1,0:T(8,128)(2,1)S(1)}, u32[]{:S(2)}, u32[]{:S(2)}) collective-permute-start(bf16[128,576]{1,0:T(8,128)(2,1)} %bitcast.15), channel_id=1, source_target_pairs={{0,16},{16,0},{1,17},{17,1},{2,18},{18,2},{3,19},{19,3},{4,20},{20... | collective-permute-start | bytes 442376 | tf_op jit(solution)/shard_map/ppermute | solution.py:193
  2.0 0.1 stack.23.where
  2.0 0.0 copy-start
  2.0 1.1 copy-done
  3.1 0.0 copy-start.1
  3.1 0.9 copy-done.1
  4.0 0.9 shard_map.46
  5.0 0.0 collective-permute-done.got_ref
  5.0 1.1 shard_map.47
  6.1 12.9 %all_to_all.25 = bf16[16,8,512]{2,1,0:T(8,128)(2,1)S(1)} all-to-all(bf16[16,8,512]{2,1,0:T(8,128)(2,1)S(1)} %bitcast.17), channel_id=1, replica_groups={{0,2,1,3,32,34,33,35,256,258,257,259,288,290,289,291},{4,6,5,7,36,38,37..., dimensions={0} | all-to-all | bytes 262144 | tf_op jit(solution)/shard_map/all_to_all | solution.py:167
  19.1 18.2 %all_to_all.26.in_ref = bf16[4,160,512]{2,1,0:T(8,128)(2,1)S(1)} all-to-all(bf16[4,160,512]{2,1,0:T(8,128)(2,1)S(1)} %shard_map.48), channel_id=1, replica_groups={{0,64,160,224},{1,65,161,225},{2,66,162,226},{3,67,163,227},{4,68,164,2..., dimensions={0} | all-to-all | bytes 1310720 | tf_op jit(solution)/shard_map/all_to_all | solution.py:167
  37.3 0.1 shard_map.49
  37.4 39.2 %all_to_all.27.own_ref = bf16[4,544,512]{2,1,0:T(8,128)(2,1)S(1)} all-to-all(bf16[4,544,512]{2,1,0:T(8,128)(2,1)S(1)} %shard_map.49), channel_id=1, replica_groups={{0,4,10,14},{1,5,11,15},{2,6,8,12},{3,7,9,13},{16,80,176,240},{17,81,17..., dimensions={0} | all-to-all | bytes 4456448 | tf_op jit(solution)/shard_map/all_to_all | solution.py:167
  76.6 1.6 broadcast_in_dim.9
  78.2 0.0 copy-start.4
  78.2 0.0 copy-start.5
  78.2 6.1 %all-to-all-start.3 = ((bf16[16,128,512]{2,1,0:T(8,128)(2,1)}), bf16[16,128,512]{2,1,0:T(8,128)(2,1)}, u32[]{:S(2)}, u32[]{:S(2)}) async-start(bf16[16,128,512]{2,1,0:T(8,128)(2,1)} %broadcast_in_dim.9), calls=%async_computation.3 | async-start | bytes 4194304 | tf_op jit(solution)/shard_map/all_to_all | solution.py:167
  84.3 1.9 %collective-permute-start.1 = (bf16[4,544,512]{2,1,0:T(8,128)(2,1)S(1)}, bf16[4,544,512]{2,1,0:T(8,128)(2,1)S(1)}, u32[]{:S(2)}, u32[]{:S(2)}) collective-permute-start(bf16[4,544,512]{2,1,0:T(8,128)(2,1)S(1)} %all_to_all.27.own_ref), channel_id=1, source_target_pairs={{0,16},{16,0},{1,17},{17,1},{2,18},{18,2},{3,19},{19,3},{4,20},{20... | collective-permute-start | bytes 6684680 | tf_op jit(solution)/shard_map/ppermute | solution.py:201
  86.2 4.3 %collective-permute-done.1.other_ref = bf16[4,544,512]{2,1,0:T(8,128)(2,1)S(1)} collective-permute-done((bf16[4,544,512]{2,1,0:T(8,128)(2,1)S(1)}, bf16[4,544,512]{2,1,0:T(8,128)(2,1)S(1)}, u32[]{:S(2)}, u32[]{:S(2)}) %collective-permute-start.1) | collective-permute-done | bytes 2228256 | tf_op jit(solution)/shard_map/ppermute | solution.py:201
  90.5 0.0 copy-start.2
  90.5 1.4 copy-done.2
  91.9 15.8 %all-to-all-done.3 = bf16[16,128,512]{2,1,0:T(8,128)(2,1)} async-done(((bf16[16,128,512]{2,1,0:T(8,128)(2,1)}), bf16[16,128,512]{2,1,0:T(8,128)(2,1)}, u32[]{:S(2)}, u32[]{:S(2)}) %all-to-all-start.3) | async-done | bytes 2097184 | tf_op jit(solution)/shard_map/all_to_all | solution.py:167
  107.7 0.0 copy-done.4
  107.7 0.0 copy-done.5
  107.7 0.0 copy-start.3
  107.7 1.6 %copy-done.3 = bf16[4,544,512]{2,1,0:T(8,128)(2,1)S(1)} copy-done((bf16[4,544,512]{2,1,0:T(8,128)(2,1)S(1)}, bf16[4,544,512]{2,1,0:T(8,128)(2,1)}, u32[]{:S(2)}) %copy-start.3) | copy-done | bytes 2228248
  109.3 6.4 %shard_map.50 = bf16[16,128,512]{2,1,0:T(8,128)(2,1)S(1)} custom-call(s32[5]{0:T(128)S(1)} %stack.23.where, f32[32]{0:T(128)S(1)} %copy-done.5, bf16[16,16,8,512]{3,2,1,0:T(8,128)(2,1)} %bitcast.9.left_ref, bf16[4,544,512]{2,1,0:T(8,128)(2,1)S(1)} %all_to_all.27.own_ref, bf16[4,544,512]{2,1,0:T(8,128)(2,1)S(1)} %copy-done.3, f32[1,512]{1,0:T(1,128)S(1)} %bitcast.18), custom_call_target="tpu_custom_call" | custom-call | flops 4294967296 | bytes 2097152 | tf_op jit(solution)/shard_map/pallas_call | solution.py:204
  115.7 28.3 %all_to_all.28.shares = bf16[16,128,512]{2,1,0:T(8,128)(2,1)S(1)} all-to-all(bf16[16,128,512]{2,1,0:T(8,128)(2,1)S(1)} %shard_map.50), channel_id=1, replica_groups=mesh['xl'=2,'y4'=4,'yb'=2,'c'=2,'z4'=4,'zb'=2,'xh'=2] {'xl','yb','xh','zb'}, dimensions={0} | all-to-all | bytes 4194304 | tf_op jit(solution)/shard_map/all_to_all | solution.py:167
  144.1 0.4 shard_map.51
  144.5 3.4 %collective-permute-start.2 = (bf16[128,512]{1,0:T(8,128)(2,1)S(1)}, bf16[128,512]{1,0:T(8,128)(2,1)S(1)}, u32[]{:S(2)}, u32[]{:S(2)}) collective-permute-start(bf16[128,512]{1,0:T(8,128)(2,1)S(1)} %shard_map.51), channel_id=1, source_target_pairs={{0,0},{1,1},{2,2},{3,3},{4,32},{5,33},{6,34},{7,35},{8,258},{9,259... | collective-permute-start | bytes 393224 | tf_op jit(solution)/shard_map/ppermute | solution.py:213
  147.9 9.8 %collective-permute-done.2 = bf16[128,512]{1,0:T(8,128)(2,1)S(1)} collective-permute-done((bf16[128,512]{1,0:T(8,128)(2,1)S(1)}, bf16[128,512]{1,0:T(8,128)(2,1)S(1)}, u32[]{:S(2)}, u32[]{:S(2)}) %collective-permute-start.2) | collective-permute-done | bytes 131104 | tf_op jit(solution)/shard_map/ppermute | solution.py:213
  157.8 1.0 copy.5
  (3 shorter events, 0.1 us)
Async XLA Ops:
  0.0 5.0 %collective-permute-start = (bf16[128,576]{1,0:T(8,128)(2,1)}, bf16[128,576]{1,0:T(8,128)(2,1)S(1)}, u32[]{:S(2)}, u32[]{:S(2)}) collective-permute-start(bf16[128,576]{1,0:T(8,128)(2,1)} %bitcast.15), channel_id=1, source_target_pairs={{0,16},{16,0},{1,17},{17,1},{2,18},{18,2},{3,19},{19,3},{4,20},{20... | collective-permute-start | bytes 442376 | tf_op jit(solution)/shard_map/ppermute | solution.py:193
  2.0 1.1 copy-start
  3.1 0.9 copy-start.1
  78.2 29.5 %copy-start.4 = (f32[512]{0:T(512)S(1)}, f32[512]{0:T(512)}, u32[]{:S(2)}) copy-start(f32[512]{0:T(512)} %param.7) | copy-start | bytes 6148
  78.2 29.5 %copy-start.5 = (f32[32]{0:T(128)S(1)}, f32[32]{0:T(128)}, u32[]{:S(2)}) copy-start(f32[32]{0:T(128)} %occ_ref.1) | copy-start | bytes 388
  78.2 29.5 %all-to-all-start.3 = ((bf16[16,128,512]{2,1,0:T(8,128)(2,1)}), bf16[16,128,512]{2,1,0:T(8,128)(2,1)}, u32[]{:S(2)}, u32[]{:S(2)}) async-start(bf16[16,128,512]{2,1,0:T(8,128)(2,1)} %broadcast_in_dim.9), calls=%async_computation.3 | async-start | bytes 4194304 | tf_op jit(solution)/shard_map/all_to_all | solution.py:167
  84.3 6.2 %collective-permute-start.1 = (bf16[4,544,512]{2,1,0:T(8,128)(2,1)S(1)}, bf16[4,544,512]{2,1,0:T(8,128)(2,1)S(1)}, u32[]{:S(2)}, u32[]{:S(2)}) collective-permute-start(bf16[4,544,512]{2,1,0:T(8,128)(2,1)S(1)} %all_to_all.27.own_ref), channel_id=1, source_target_pairs={{0,16},{16,0},{1,17},{17,1},{2,18},{18,2},{3,19},{19,3},{4,20},{20... | collective-permute-start | bytes 6684680 | tf_op jit(solution)/shard_map/ppermute | solution.py:201
  90.5 1.4 copy-start.2
  107.7 1.6 %copy-start.3 = (bf16[4,544,512]{2,1,0:T(8,128)(2,1)S(1)}, bf16[4,544,512]{2,1,0:T(8,128)(2,1)}, u32[]{:S(2)}) copy-start(bf16[4,544,512]{2,1,0:T(8,128)(2,1)} %copy-done.2) | copy-start | bytes 6684676
  144.5 13.3 %collective-permute-start.2 = (bf16[128,512]{1,0:T(8,128)(2,1)S(1)}, bf16[128,512]{1,0:T(8,128)(2,1)S(1)}, u32[]{:S(2)}, u32[]{:S(2)}) collective-permute-start(bf16[128,512]{1,0:T(8,128)(2,1)S(1)} %shard_map.51), channel_id=1, source_target_pairs={{0,0},{1,1},{2,2},{3,3},{4,32},{5,33},{6,34},{7,35},{8,258},{9,259... | collective-permute-start | bytes 393224 | tf_op jit(solution)/shard_map/ppermute | solution.py:213

commit v4 on v3

--- a/solution.py
+++ b/solution.py
@@ -15,6 +15,7 @@
 MIB = 1 << 20
 VMEM = pl.BlockSpec(memory_space=pltpu.VMEM)
 SMEM = pl.BlockSpec(memory_space=pltpu.SMEM)
+ANY = pl.BlockSpec(memory_space=pl.ANY)
 
 
 def exact_rows(source_row, rows):
@@ -62,11 +63,14 @@
             out_ref[target, 512 + 8 * source : 520 + 8 * source, :] = in_ref[source, at : at + 8, :]
 
 
-def density_kernel(where, occ_ref, left_ref, own_ref, other_ref, vir_ref, out_ref, coulomb, total):
+def density_kernel(where, occ_ref, left_ref, own_ref, other_in, vir_ref, out_ref, coulomb, total, other_ref, arrived):
     core = where[3]
+    fetch = pltpu.make_async_copy(other_in, other_ref, arrived)
+    fetch.start()
     down = jnp.broadcast_to(vir_ref[...], (512, 512))
     total[...] = down.T + down
     coulomb[...] = jnp.zeros_like(coulomb)
+    fetch.wait()
 
     def own(second):
         return own_ref[second, 0:512, :]
@@ -110,14 +114,14 @@
     out_ref[...] = exact_rows(source_row, total.astype(jnp.bfloat16))
 
 
-def call(kernel, shapes, specs, scratch=(), flops=0):
+def call(kernel, shapes, specs, scratch=(), flops=0, vmem=24):
     return pl.pallas_call(
         kernel,
         out_shape=[jax.ShapeDtypeStruct(shape, jnp.bfloat16) for shape in shapes],
         in_specs=specs,
         out_specs=[VMEM] * len(shapes),
         scratch_shapes=list(scratch),
-        compiler_params=pltpu.CompilerParams(vmem_limit_bytes=24 * MIB),
+        compiler_params=pltpu.CompilerParams(vmem_limit_bytes=vmem * MIB),
         cost_estimate=pl.CostEstimate(flops=flops, bytes_accessed=2 * MIB, transcendentals=0),
     )
 
@@ -204,9 +208,15 @@
     (partial,) = call(
         density_kernel,
         [(16, 128, 512)],
-        [SMEM, SMEM, VMEM, VMEM, VMEM, VMEM],
-        [pltpu.VMEM((2, 512, 512), jnp.float32), pltpu.VMEM((512, 512), jnp.float32)],
+        [SMEM, SMEM, VMEM, VMEM, ANY, VMEM],
+        [
+            pltpu.VMEM((2, 512, 512), jnp.float32),
+            pltpu.VMEM((512, 512), jnp.float32),
+            pltpu.VMEM((4, 544, 512), jnp.bfloat16),
+            pltpu.SemaphoreType.DMA,
+        ],
         flops=4 * 512 * 1024 * 2048,
+        vmem=58,
     )(where, occ_energy, left.reshape(16, 16, 8, 512), own, other, vir_energy.reshape(1, 512))
     shares = exchange(partial, COMPACT)
     (summed,) = call(sum_kernel, [(128, 512)], [VMEM])(shares)

time: 159 us -> 162 us (1.019)
  Pallas kernels: 9.11 us -> 12.8 us
  local copies, waits for them, and re-layouts: 7.62 us -> 4.79 us
    pallas_call x1, Pallas kernels: 6.45 us -> 10.1 us  [body(): call(density_kernel, [(16, 128, 512)], [SMEM, SMEM, VMEM, VMEM, ANY, VMEM...]
    unnamed x12 -> x8, local copies, waits for them, and re-layouts: 4.99 us -> 1.99 us
where the time goes in v4:
time: 162 us; the launch traced here: 161 us
  blocking collectives  98.8 us (61%)
  waiting for transfers between devices  31.3 us (19%)
  starting transfers between devices  13.3 us (8%)
  Pallas kernels  12.8 us (8%)
  local copies, waits for them, and re-layouts  4.79 us (3%)
    all_to_all x4, blocking collectives, exchange(): lax.all_to_all(rows, axes, split_axis=0, concat_axis=0, axis_index_groups...  98.8 us
    all_to_all x1, waiting for transfers between devices, exchange(): lax.all_to_all(rows, axes, split_axis=0, concat_axis=0, axis_index_groups...  17 us
    pallas_call x1, Pallas kernels, body(): call(density_kernel, [(16, 128, 512)], [SMEM, SMEM, VMEM, VMEM, ANY, VMEM...  10.1 us
    ppermute x1, waiting for transfers between devices, body(): placed = lax.ppermute(summed, AXES, to_place())  9.83 us
    all_to_all x1, starting transfers between devices, exchange(): lax.all_to_all(rows, axes, split_axis=0, concat_axis=0, axis_index_groups...  5.99 us
    ppermute x1, waiting for transfers between devices, body(): other = lax.ppermute(own, 'c', [(0, 1), (1, 0)])  4.44 us
    ppermute x1, starting transfers between devices, body(): placed = lax.ppermute(summed, AXES, to_place())  3.44 us
  transfers between devices with their start and end apart: 4, of which 3 were waited for; matrix products, arithmetic and copies ran while one was open for 0% of the time, Pallas kernels for 1%

profile of v4, /device:TPU:66, one launch (start us, length us, event | category | flops | bytes accessed | tf_op | source)
XLA Modules:
  0.0 161.1 jit_solution(10538781270837574243)
XLA Ops:
  0.0 1.9 %collective-permute-start = (bf16[128,576]{1,0:T(8,128)(2,1)}, bf16[128,576]{1,0:T(8,128)(2,1)S(1)}, u32[]{:S(2)}, u32[]{:S(2)}) collective-permute-start(bf16[128,576]{1,0:T(8,128)(2,1)} %bitcast.15), channel_id=1, source_target_pairs={{0,16},{16,0},{1,17},{17,1},{2,18},{18,2},{3,19},{19,3},{4,20},{20... | collective-permute-start | bytes 442376 | tf_op jit(solution)/shard_map/ppermute | solution.py:197
  2.0 0.1 stack.23.where
  2.0 0.0 copy-start
  2.0 1.1 copy-done
  3.1 0.0 copy-start.1
  3.1 0.9 copy-done.1
  4.0 0.0 copy-start.2
  4.0 0.9 shard_map.46
  5.0 0.0 collective-permute-done.got_ref
  5.0 1.1 shard_map.47
  6.1 12.9 %all_to_all.25 = bf16[16,8,512]{2,1,0:T(8,128)(2,1)S(1)} all-to-all(bf16[16,8,512]{2,1,0:T(8,128)(2,1)S(1)} %bitcast.17), channel_id=1, replica_groups={{0,2,1,3,32,34,33,35,256,258,257,259,288,290,289,291},{4,6,5,7,36,38,37..., dimensions={0} | all-to-all | bytes 262144 | tf_op jit(solution)/shard_map/all_to_all | solution.py:171
  19.1 18.2 %all_to_all.26.in_ref = bf16[4,160,512]{2,1,0:T(8,128)(2,1)S(1)} all-to-all(bf16[4,160,512]{2,1,0:T(8,128)(2,1)S(1)} %shard_map.48), channel_id=1, replica_groups={{0,64,160,224},{1,65,161,225},{2,66,162,226},{3,67,163,227},{4,68,164,2..., dimensions={0} | all-to-all | bytes 1310720 | tf_op jit(solution)/shard_map/all_to_all | solution.py:171
  37.3 0.1 shard_map.49
  37.5 0.0 copy-done.2
  37.5 39.1 %all_to_all.27.own_ref = bf16[4,544,512]{2,1,0:T(8,128)(2,1)S(1)} all-to-all(bf16[4,544,512]{2,1,0:T(8,128)(2,1)S(1)} %shard_map.49), channel_id=1, replica_groups={{0,4,10,14},{1,5,11,15},{2,6,8,12},{3,7,9,13},{16,80,176,240},{17,81,17..., dimensions={0} | all-to-all | bytes 4456448 | tf_op jit(solution)/shard_map/all_to_all | solution.py:171
  76.6 0.0 copy-start.3
  76.6 1.7 %broadcast_in_dim.9 = bf16[16,128,512]{2,1,0:T(8,128)(2,1)} broadcast(bf16[128,512]{1,0:T(8,128)(2,1)S(1)} %bitcast.18), dimensions={1,2} | broadcast | bytes 2228224 | tf_op jit(solution)/shard_map/broadcast_in_dim | solution.py:206
  78.4 6.0 %all-to-all-start.3 = ((bf16[16,128,512]{2,1,0:T(8,128)(2,1)}), bf16[16,128,512]{2,1,0:T(8,128)(2,1)}, u32[]{:S(2)}, u32[]{:S(2)}) async-start(bf16[16,128,512]{2,1,0:T(8,128)(2,1)} %broadcast_in_dim.9), calls=%async_computation.3 | async-start | bytes 4194304 | tf_op jit(solution)/shard_map/all_to_all | solution.py:171
  84.4 0.0 copy-done.3
  84.4 1.9 %collective-permute-start.1 = (bf16[4,544,512]{2,1,0:T(8,128)(2,1)S(1)}, bf16[4,544,512]{2,1,0:T(8,128)(2,1)}, u32[]{:S(2)}, u32[]{:S(2)}) collective-permute-start(bf16[4,544,512]{2,1,0:T(8,128)(2,1)S(1)} %all_to_all.27.own_ref), channel_id=1, source_target_pairs={{0,16},{16,0},{1,17},{17,1},{2,18},{18,2},{3,19},{19,3},{4,20},{20... | collective-permute-start | bytes 6684680 | tf_op jit(solution)/shard_map/ppermute | solution.py:205
  86.3 4.4 %collective-permute-done.1.other_in = bf16[4,544,512]{2,1,0:T(8,128)(2,1)} collective-permute-done((bf16[4,544,512]{2,1,0:T(8,128)(2,1)S(1)}, bf16[4,544,512]{2,1,0:T(8,128)(2,1)}, u32[]{:S(2)}, u32[]{:S(2)}) %collective-permute-start.1) | collective-permute-done | bytes 2228256 | tf_op jit(solution)/shard_map/ppermute | solution.py:205
  90.7 17.0 %all-to-all-done.3 = bf16[16,128,512]{2,1,0:T(8,128)(2,1)} async-done(((bf16[16,128,512]{2,1,0:T(8,128)(2,1)}), bf16[16,128,512]{2,1,0:T(8,128)(2,1)}, u32[]{:S(2)}, u32[]{:S(2)}) %all-to-all-start.3) | async-done | bytes 2097184 | tf_op jit(solution)/shard_map/all_to_all | solution.py:171
  107.7 10.1 %shard_map.50 = bf16[16,128,512]{2,1,0:T(8,128)(2,1)} custom-call(s32[5]{0:T(128)} %copy-done.2, f32[32]{0:T(128)} %occ_ref.1, bf16[16,16,8,512]{3,2,1,0:T(8,128)(2,1)} %bitcast.9.left_ref, bf16[4,544,512]{2,1,0:T(8,128)(2,1)} %copy-done.3, bf16[4,544,512]{2,1,0:T(8,128)(2,1)} %collective-permute-done.1.other_in, f32[1,512]{1,0:T(1,128)} %bitcast.19), custom_call_target="tpu_custom_call" | custom-call | flops 4294967296 | bytes 2097152 | tf_op jit(solution)/shard_map/pallas_call | solution.py:208
  117.8 28.5 %all_to_all.28.shares = bf16[16,128,512]{2,1,0:T(8,128)(2,1)S(1)} all-to-all(bf16[16,128,512]{2,1,0:T(8,128)(2,1)} %shard_map.50), channel_id=1, replica_groups=mesh['xl'=2,'y4'=4,'yb'=2,'c'=2,'z4'=4,'zb'=2,'xh'=2] {'xl','yb','xh','zb'}, dimensions={0} | all-to-all | bytes 4194304 | tf_op jit(solution)/shard_map/all_to_all | solution.py:171
  146.3 0.4 shard_map.51
  146.8 3.4 %collective-permute-start.2 = (bf16[128,512]{1,0:T(8,128)(2,1)S(1)}, bf16[128,512]{1,0:T(8,128)(2,1)S(1)}, u32[]{:S(2)}, u32[]{:S(2)}) collective-permute-start(bf16[128,512]{1,0:T(8,128)(2,1)S(1)} %shard_map.51), channel_id=1, source_target_pairs={{0,0},{1,1},{2,2},{3,3},{4,32},{5,33},{6,34},{7,35},{8,258},{9,259... | collective-permute-start | bytes 393224 | tf_op jit(solution)/shard_map/ppermute | solution.py:223
  150.2 9.8 %collective-permute-done.2 = bf16[128,512]{1,0:T(8,128)(2,1)S(1)} collective-permute-done((bf16[128,512]{1,0:T(8,128)(2,1)S(1)}, bf16[128,512]{1,0:T(8,128)(2,1)S(1)}, u32[]{:S(2)}, u32[]{:S(2)}) %collective-permute-start.2) | collective-permute-done | bytes 131104 | tf_op jit(solution)/shard_map/ppermute | solution.py:223
  160.1 1.0 copy.5
  (3 shorter events, 0.1 us)
Async XLA Ops:
  0.0 5.0 %collective-permute-start = (bf16[128,576]{1,0:T(8,128)(2,1)}, bf16[128,576]{1,0:T(8,128)(2,1)S(1)}, u32[]{:S(2)}, u32[]{:S(2)}) collective-permute-start(bf16[128,576]{1,0:T(8,128)(2,1)} %bitcast.15), channel_id=1, source_target_pairs={{0,16},{16,0},{1,17},{17,1},{2,18},{18,2},{3,19},{19,3},{4,20},{20... | collective-permute-start | bytes 442376 | tf_op jit(solution)/shard_map/ppermute | solution.py:197
  2.0 1.1 copy-start
  3.1 0.9 copy-start.1
  4.0 33.4 %copy-start.2 = (s32[5]{0:T(128)}, s32[5]{0:T(128)S(1)}, u32[]{:S(2)}) copy-start(s32[5]{0:T(128)S(1)} %stack.23.where) | copy-start | bytes 64
  76.6 7.7 %copy-start.3 = (bf16[4,544,512]{2,1,0:T(8,128)(2,1)}, bf16[4,544,512]{2,1,0:T(8,128)(2,1)S(1)}, u32[]{:S(2)}) copy-start(bf16[4,544,512]{2,1,0:T(8,128)(2,1)S(1)} %all_to_all.27.own_ref) | copy-start | bytes 6684676
  78.4 29.4 %all-to-all-start.3 = ((bf16[16,128,512]{2,1,0:T(8,128)(2,1)}), bf16[16,128,512]{2,1,0:T(8,128)(2,1)}, u32[]{:S(2)}, u32[]{:S(2)}) async-start(bf16[16,128,512]{2,1,0:T(8,128)(2,1)} %broadcast_in_dim.9), calls=%async_computation.3 | async-start | bytes 4194304 | tf_op jit(solution)/shard_map/all_to_all | solution.py:171
  84.4 6.4 %collective-permute-start.1 = (bf16[4,544,512]{2,1,0:T(8,128)(2,1)S(1)}, bf16[4,544,512]{2,1,0:T(8,128)(2,1)}, u32[]{:S(2)}, u32[]{:S(2)}) collective-permute-start(bf16[4,544,512]{2,1,0:T(8,128)(2,1)S(1)} %all_to_all.27.own_ref), channel_id=1, source_target_pairs={{0,16},{16,0},{1,17},{17,1},{2,18},{18,2},{3,19},{19,3},{4,20},{20... | collective-permute-start | bytes 6684680 | tf_op jit(solution)/shard_map/ppermute | solution.py:205
  146.8 13.3 %collective-permute-start.2 = (bf16[128,512]{1,0:T(8,128)(2,1)S(1)}, bf16[128,512]{1,0:T(8,128)(2,1)S(1)}, u32[]{:S(2)}, u32[]{:S(2)}) collective-permute-start(bf16[128,512]{1,0:T(8,128)(2,1)S(1)} %shard_map.51), channel_id=1, source_target_pairs={{0,0},{1,1},{2,2},{3,3},{4,32},{5,33},{6,34},{7,35},{8,258},{9,259... | collective-permute-start | bytes 393224 | tf_op jit(solution)/shard_map/ppermute | solution.py:223
